TPU v7x, 32 devices: a whole 2x2x4 slice. The times are simulated.
32 devices in a mesh: groups: 2 (over y), tile: 16 (over z, x, core).
Axes of the slice: x: 2, y: 2, z: 4, core: 2. Of those that a mesh axis runs over, the one named last changes fastest.
Arguments:
- features: bfloat16 [192, 16, 16, 256], P(('groups', 'tile')), parts along dimension 0, may hold values from -6 to 6
- weights: bfloat16 [9, 256, 256], replicated, may hold values from -0.125 to 0.125
- grad_out: bfloat16 [192, 16, 16, 256], P(('groups', 'tile')), parts along dimension 0, may hold values from -6 to 6
- tile_pos: int32 [192], P(('groups', 'tile')), parts along dimension 0, may hold values from -1 to 7, as said below
- neighbours: int32 [192, 8], P(('groups', 'tile')), parts along dimension 0, may hold values from -1 to 15, as said below
Outputs:
- activation: bfloat16 [192, 16, 16, 256], P(('groups', 'tile')), parts along dimension 0
- weight_grad: float32 [18, 256, 256], P('groups'), parts along dimension 0
- input_grad: bfloat16 [192, 16, 16, 256], P(('groups', 'tile')), parts along dimension 0
There are 2 independent parts, one for each index of `groups`. A program takes and returns all parts, laid end to end along the dimension named above; an argument that names none is the same for every part. Nothing has to cross between parts.
Inputs may be any that keep to these rules, and one draw needn't show every extreme that they name: `tile_pos`: each device's 6 slots hold the tissue tiles of its band of 2 x 4 tiles first, in raster order, then empty slots; every device holds 2 or more tissue tiles and at least one device holds 6. A code c names slot c % 6 of the device whose index is the own index plus c // 6 - 1; codes of left and right neighbours name the own device, up and up-diagonal neighbours lie on the own or the preceding device, down and down-diagonal ones on the own or the following device. Neighbours are tissue tiles of the slide's grid and the relation is symmetric; empty slots and missing neighbours have -1.
All inputs are finite; a program needn't handle non-finite values.
Results may differ from a plain program's by a relative error of at most 0.0049.
Values may be sent and summed in bfloat16 or wider, within the bound.
No kernel may reach another device: no remote copies, remote signals or barrier semaphores. Data moves between devices by JAX's collectives and lax.ppermute only.
A program may use at most 64 MiB of HBM per device.

v0:
```python
import math
import jax
import jax.numpy as jnp
from jax import lax
from jax.sharding import PartitionSpec as P

EDGE_PICK = (1, 0, 3, 2, 1, 1, 0, 0)
ROOT_HALF = 0.7071067811865476
INV_ROOT_TAU = 0.3989422804014327


def from_behind(value, axis, steps):
    count = lax.axis_size(axis)
    initial, last = (max(0, -steps), min(count, count - steps))
    return lax.ppermute(value, axis, [(source, source + steps) for source in range(initial, last)])


def gelu_value(preact):
    return preact * (0.5 * (1.0 + lax.erf(preact * ROOT_HALF)))


def gelu_slope(preact):
    cumulative = 0.5 * (1.0 + lax.erf(preact * ROOT_HALF))
    density = jnp.exp(-0.5 * preact * preact) * INV_ROOT_TAU
    return cumulative + preact * density


def edge_rims(field_map):
    return jnp.stack(
        [field_map[:, 0], field_map[:, -1], field_map[:, :, 0], field_map[:, :, -1]], axis=1
    )


def surround(center, gathered):
    upper_row = jnp.concatenate([gathered[:, 4, -1:], gathered[:, 0], gathered[:, 5, :1]], axis=1)
    lower_row = jnp.concatenate([gathered[:, 6, -1:], gathered[:, 1], gathered[:, 7, :1]], axis=1)
    middle = jnp.concatenate(
        [gathered[:, 2][:, :, None], center, gathered[:, 3][:, :, None]], axis=2
    )
    return jnp.concatenate([upper_row[:, None], middle, lower_row[:, None]], axis=1)


def tap_matrix(extended, flipped):
    side_cells = extended.shape[1] - 2
    pieces = []
    for row_tap in range(3):
        for col_tap in range(3):
            row_start = 2 - row_tap if flipped else row_tap
            col_start = 2 - col_tap if flipped else col_tap
            pieces.append(
                extended[:, row_start : row_start + side_cells, col_start : col_start + side_cells]
            )
    stacked = jnp.concatenate(pieces, axis=-1)
    return stacked.reshape(-1, stacked.shape[-1])


def lookup(edge_table, source, linked):
    clipped = jnp.clip(jnp.where(linked, source, 0), 0, edge_table.shape[0] - 1)
    picked = jnp.take(edge_table, clipped.reshape(-1), axis=0).reshape(
        linked.shape + edge_table.shape[1:]
    )
    return jnp.where(linked[:, :, None, None], picked, jnp.zeros((), picked.dtype))


def narrow_sources(neighbours, edge_picks, tile_dev):
    anchor = neighbours // tile_dev
    own_slot = (neighbours - tile_dev) * 4 + edge_picks[None, :]
    return jnp.where(
        anchor == 1,
        own_slot,
        jnp.where(anchor == 0, 4 * tile_dev + neighbours, 3 * tile_dev + neighbours),
    )


def narrow_table(own_rims, upper_rows, lower_rows):
    tile_dev = own_rims.shape[0]
    side_cells = own_rims.shape[2]
    channels = own_rims.shape[3]
    return jnp.concatenate(
        [own_rims.reshape(4 * tile_dev, side_cells, channels), upper_rows, lower_rows], axis=0
    )


def forward_tiles(extended, grad_tiles, tissue_gate, weight_mat):
    tile_count = extended.shape[0]
    side_cells = extended.shape[1] - 2
    channels = weight_mat.shape[1]
    preact = jnp.dot(tap_matrix(extended, False), weight_mat, preferred_element_type=jnp.float32)
    preact = preact.reshape(tile_count, side_cells, side_cells, channels)
    gate_cells = tissue_gate[:, None, None, None]
    act_map = (gelu_value(preact) * gate_cells).astype(jnp.bfloat16)
    slope_map = (grad_tiles.astype(jnp.float32) * gelu_slope(preact) * gate_cells).astype(
        jnp.bfloat16
    )
    return (act_map, slope_map)


def weight_terms(ext_x, slope_map):
    return lax.dot_general(
        tap_matrix(ext_x, False),
        slope_map.reshape(-1, slope_map.shape[-1]),
        (((0,), (0,)), ((), ())),
        preferred_element_type=jnp.float32,
    )


def backward_tiles(ext_g, tissue_gate, flip_mat):
    tile_count = ext_g.shape[0]
    side_cells = ext_g.shape[1] - 2
    channels = flip_mat.shape[1]
    back_map = jnp.dot(tap_matrix(ext_g, True), flip_mat, preferred_element_type=jnp.float32)
    back_map = (
        back_map.reshape(tile_count, side_cells, side_cells, channels)
        * tissue_gate[:, None, None, None]
    )
    return back_map.astype(jnp.bfloat16)


def body(features, weights, grad_out, tile_pos, neighbours):
    tile_dev = features.shape[0]
    side_cells = features.shape[1]
    channels = features.shape[3]
    devices = lax.axis_size("tile")
    tissue = (tile_pos >= 0).astype(jnp.float32)
    weight_mat = weights.reshape(9 * channels, channels)
    flip_mat = jnp.transpose(weights, (0, 2, 1)).reshape(9 * channels, channels)
    edge_picks = jnp.array(EDGE_PICK, dtype=jnp.int32)
    linked = neighbours >= 0
    rims_x = edge_rims(features)
    from_above = from_behind(rims_x[:, 1], "tile", 1)
    from_below = from_behind(rims_x[:, 0], "tile", -1)
    table_x = narrow_table(rims_x, from_above, from_below)
    source = narrow_sources(neighbours, edge_picks, tile_dev)
    ext_x = surround(features, lookup(table_x, source, linked))
    activation, pre_grad = forward_tiles(ext_x, grad_out, tissue, weight_mat)
    rims_g = edge_rims(pre_grad)
    grad_above = from_behind(rims_g[:, 1], "tile", 1)
    grad_below = from_behind(rims_g[:, 0], "tile", -1)
    table_g = narrow_table(rims_g, grad_above, grad_below)
    ext_g = surround(pre_grad, lookup(table_g, source, linked))
    weight_part = weight_terms(ext_x, pre_grad)
    grad_scale = 1.0 / math.sqrt(tile_dev * devices * side_cells * side_cells)
    summed = lax.psum(weight_part, "tile")
    weight_grad = (summed * grad_scale).reshape(9, channels, channels)
    input_grad = backward_tiles(ext_g, tissue, flip_mat)
    return (activation, weight_grad, input_grad)


def solution(mesh):
    in_specs = (
        P(("groups", "tile"), None, None, None),
        P(),
        P(("groups", "tile"), None, None, None),
        P(("groups", "tile")),
        P(("groups", "tile"), None),
    )
    out_specs = (
        P(("groups", "tile"), None, None, None),
        P("groups", None, None),
        P(("groups", "tile"), None, None, None),
    )
    return jax.shard_map(body, mesh=mesh, in_specs=in_specs, out_specs=out_specs, check_vma=False)
```

profile of v0, /device:TPU:0, one launch (start us, length us, event | category | flops | bytes accessed | tf_op | source)
XLA Modules:
  0.0 143.3 jit_solution(6044019779046628402)
XLA Ops:
  7.2 0.9 slice_bitcast_fusion.11
  8.2 1.3 collective-permute-start.1
  9.5 3.0 %collective-permute-start = (bf16[6,16,256]{2,1,0:T(8,128)(2,1)S(1)}, bf16[6,16,256]{2,1,0:T(8,128)(2,1)S(1)}, u32[]{:S(2)}, u32[]{:S(2)}) collective-permute-start(bf16[6,16,256]{2,1,0:T(8,128)(2,1)S(1)} %get-tuple-element.18), channel_id=1, source_target_pairs={{0,1},{1,2},{2,3},{3,4},{4,5},{5,6},{6,7},{7,8},{8,9},{9,10},{10,1... | collective-permute-start | bytes 147464 | tf_op jit(solution)/shard_map/ppermute | solution.py:15
  12.5 1.3 fusion.14
  13.8 0.7 select_clamp_fusion
  14.6 0.7 broadcast_compare_fusion
  15.3 0.7 compare_convert_fusion
  16.1 1.6 %copy.89 = bf16[9,256,256]{1,2,0:T(8,128)(2,1)} copy(bf16[9,256,256]{2,1,0:T(8,128)(2,1)S(1)} %copy-done.1) | data formatting | bytes 2359296 | tf_op args[1]
  17.8 0.6 gather_fusion
  18.9 1.2 pad_maximum_fusion
  21.3 0.5 fusion.9
  22.5 0.4 copy-done.3
  22.9 3.6 %fusion.6 = (bf16[6,16,16,256]{3,2,1,0:T(8,128)(2,1)S(1)}, bf16[6,16,16,256]{3,2,1,0:T(8,128)(2,1)}) fusion(bf16[6,16,16,256]{3,2,1,0:T(8,128)(2,1)S(1)} %copy-done.3, f32[6]{0:T(128)S(1)} %compare_convert_fusion, bf16[6,16,16,2304]{3,2,1,0:T(8,128)(2,1)S(1)} %slice_dynamic-update-slice_fusion.6, bf16[2304,256,1,1]{1,0,3,2:T(8,128)(2,1)S(1)} %bitcast.104), kind=kOutput, calls=%fused_computation.10 | convolution fusion | flops 1817837568 | bytes 10616856 | tf_op jit(solution)/shard_map/dot_general | solution.py:88
  26.5 3.5 %convolution_bitcast_fusion = f32[2304,256]{1,0:T(8,128)} fusion(bf16[6,16,16,2304]{3,2,1,0:T(8,128)(2,1)S(1)} %slice_dynamic-update-slice_fusion.6, bf16[6,16,16,256]{3,2,1,0:T(8,128)(2,1)S(1)} %get-tuple-element.4), kind=kOutput, calls=%fused_computation.2 | convolution fusion | flops 1811939328 | bytes 10223616 | tf_op jit(solution)/shard_map/dot_general | solution.py:99
  30.2 1.3 collective-permute-start.3
  31.5 5.3 %collective-permute-start.2 = (bf16[6,16,256]{2,1,0:T(8,128)(2,1)S(1)}, bf16[6,16,256]{2,1,0:T(8,128)(2,1)S(1)}, u32[]{:S(2)}, u32[]{:S(2)}) collective-permute-start(bf16[6,16,256]{2,1,0:T(8,128)(2,1)S(1)} %get-tuple-element.12), channel_id=1, source_target_pairs={{0,1},{1,2},{2,3},{3,4},{4,5},{5,6},{6,7},{7,8},{8,9},{9,10},{10,1... | collective-permute-start | bytes 147464 | tf_op jit(solution)/shard_map/ppermute | solution.py:15
  36.9 0.6 collective-permute-done.2
  37.6 0.6 gather_fusion.1
  38.7 1.2 maximum_maximum_fusion.1
  40.6 0.5 fusion.8
  42.2 0.5 copy-done.2
  42.8 3.0 %multiply_convert_fusion = bf16[6,16,16,256]{3,2,1,0:T(8,128)(2,1)} fusion(bf16[6,16,16,2304]{3,2,1,0:T(8,128)(2,1)S(1)} %slice_dynamic-update-slice_fusion, bf16[2304,256,1,1]{1,0,3,2:T(8,128)(2,1)S(1)} %bitcast.105, f32[6]{0:T(128)S(1)} %compare_convert_fusion), kind=kOutput, calls=%fused_computation.11 | convolution fusion | flops 1812725760 | bytes 9043992 | tf_op jit(solution)/shard_map/dot_general | solution.py:111
  45.7 87.5 %all-reduce.2.cloned.1.call-done = f32[2304,256]{1,0:T(8,128)} async-done(((f32[2304,256]{1,0:T(8,128)}), f32[2304,256]{1,0:T(8,128)}) %all-reduce.2.cloned.1.call-update) | async-done | bytes 2359312 | tf_op jit(solution)/shard_map/psum | solution.py:143
  133.2 3.3 %broadcast_multiply_fusion = f32[2304,256]{1,0:T(8,128)} fusion(f32[2304,256]{1,0:T(8,128)} %all-reduce.2.cloned.1.call-done), kind=kLoop, calls=%fused_computation.18 | loop fusion | flops 589824 | bytes 4718592 | tf_op jit(solution)/shard_map/mul | solution.py:144
  (58 shorter events, 5.3 us)
Async XLA Ops:
  7.2 9.0 %copy-start.1 = (bf16[9,256,256]{2,1,0:T(8,128)(2,1)S(1)}, bf16[9,256,256]{2,1,0:T(8,128)(2,1)}, u32[]{:S(2)}) copy-start(bf16[9,256,256]{2,1,0:T(8,128)(2,1)} %param.9) | copy-start | bytes 3538948
  7.2 126.0 %all-reduce.2.cloned.1.call-start = ((), (), s32[]{:S(2)}) async-start(), calls=%async_computation | async-start | bytes 4718592 | tf_op jit(solution)/shard_map/psum | solution.py:143
  8.2 9.6 %collective-permute-start.1 = (bf16[6,16,256]{2,1,0:T(8,128)(2,1)S(1)}, bf16[6,16,256]{2,1,0:T(8,128)(2,1)S(1)}, u32[]{:S(2)}, u32[]{:S(2)}) collective-permute-start(bf16[6,16,256]{2,1,0:T(8,128)(2,1)S(1)} %get-tuple-element.17), channel_id=1, source_target_pairs={{1,0},{2,1},{3,2},{4,3},{5,4},{6,5},{7,6},{8,7},{9,8},{10,9},{11,1... | collective-permute-start | bytes 147464 | tf_op jit(solution)/shard_map/ppermute | solution.py:15
  9.5 8.3 %collective-permute-start = (bf16[6,16,256]{2,1,0:T(8,128)(2,1)S(1)}, bf16[6,16,256]{2,1,0:T(8,128)(2,1)S(1)}, u32[]{:S(2)}, u32[]{:S(2)}) collective-permute-start(bf16[6,16,256]{2,1,0:T(8,128)(2,1)S(1)} %get-tuple-element.18), channel_id=1, source_target_pairs={{0,1},{1,2},{2,3},{3,4},{4,5},{5,6},{6,7},{7,8},{8,9},{9,10},{10,1... | collective-permute-start | bytes 147464 | tf_op jit(solution)/shard_map/ppermute | solution.py:15
  17.7 1.2 copy-start
  21.8 1.1 copy-start.3
  30.2 6.7 %collective-permute-start.3 = (bf16[6,16,256]{2,1,0:T(8,128)(2,1)S(1)}, bf16[6,16,256]{2,1,0:T(8,128)(2,1)S(1)}, u32[]{:S(2)}, u32[]{:S(2)}) collective-permute-start(bf16[6,16,256]{2,1,0:T(8,128)(2,1)S(1)} %get-tuple-element.11), channel_id=1, source_target_pairs={{1,0},{2,1},{3,2},{4,3},{5,4},{6,5},{7,6},{8,7},{9,8},{10,9},{11,1... | collective-permute-start | bytes 147464 | tf_op jit(solution)/shard_map/ppermute | solution.py:15
  31.5 6.0 %collective-permute-start.2 = (bf16[6,16,256]{2,1,0:T(8,128)(2,1)S(1)}, bf16[6,16,256]{2,1,0:T(8,128)(2,1)S(1)}, u32[]{:S(2)}, u32[]{:S(2)}) collective-permute-start(bf16[6,16,256]{2,1,0:T(8,128)(2,1)S(1)} %get-tuple-element.12), channel_id=1, source_target_pairs={{0,1},{1,2},{2,3},{3,4},{4,5},{5,6},{6,7},{7,8},{8,9},{9,10},{10,1... | collective-permute-start | bytes 147464 | tf_op jit(solution)/shard_map/ppermute | solution.py:15
  41.5 1.3 copy-start.2
Sparse Core Ops, SparseCore 0:
  30.4 102.8 all-reduce.1
where the time goes:
time: 144 us; the launch traced here: 143 us
  waiting for transfers between devices  88.1 us (61%)
  between operations  14.4 us (10%)
  starting transfers between devices  11 us (8%)
  other arithmetic  10.2 us (7%)
  matrix products  10 us (7%)
  local copies, waits for them, and re-layouts  9.6 us (7%)
    psum x1, waiting for transfers between devices, body(): summed = lax.psum(weight_part, 'tile')  87.5 us
    ppermute x4, starting transfers between devices, from_behind(): lax.ppermute(value, axis, [(source, source + steps) for source in range(i...  10.9 us
    unnamed x24, local copies, waits for them, and re-layouts  5.97 us
    dot_general x1, matrix products, forward_tiles(): jnp.dot(tap_matrix(extended, False), weight_mat, preferred_element_type=j...  3.56 us
    dot_general x1, matrix products, weight_terms(): lax.dot_general(tap_matrix(ext_x, False), slope_map.reshape(-1, slope_map...  3.52 us
    mul x1, other arithmetic, body(): weight_grad = (summed * grad_scale).reshape(9, channels, channels)  3.27 us
    dot_general x1, matrix products, backward_tiles(): jnp.dot(tap_matrix(ext_g, True), flip_mat, preferred_element_type=jnp.flo...  2.96 us
  transfers between devices with their start and end apart: 5, of which 2 were waited for; matrix products, arithmetic and copies ran while one was open for 9% of the time, Pallas kernels for 0%

commit v1 on v0

--- a/solution.py
+++ b/solution.py
@@ -140,7 +140,7 @@
     ext_g = surround(pre_grad, lookup(table_g, source, linked))
     weight_part = weight_terms(ext_x, pre_grad)
     grad_scale = 1.0 / math.sqrt(tile_dev * devices * side_cells * side_cells)
-    summed = lax.psum(weight_part, "tile")
+    summed = jnp.sum(lax.all_gather(weight_part, "tile"), axis=0)
     weight_grad = (summed * grad_scale).reshape(9, channels, channels)
     input_grad = backward_tiles(ext_g, tissue, flip_mat)
     return (activation, weight_grad, input_grad)

time: 144 us -> 244 us (1.69)
  waiting for transfers between devices: 88.1 us -> 178 us
  other arithmetic: 10.2 us -> 22 us
    all_gather x0 -> x1, waiting for transfers between devices: none -> 175 us  [body(): summed = jnp.sum(lax.all_gather(weight_part, 'tile'), axis=0)]
    psum x1 -> x0, waiting for transfers between devices: 87.5 us -> none  [body(): summed = lax.psum(weight_part, 'tile')]
    reduce_sum x0 -> x1, other arithmetic: none -> 13.5 us  [body(): summed = jnp.sum(lax.all_gather(weight_part, 'tile'), axis=0)]
    ppermute x4, waiting for transfers between devices: 0.61 us -> 3.11 us  [from_behind(): lax.ppermute(value, axis, [(source, source + steps) for source in range(i...]
    unnamed x24 -> x22, local copies, waits for them, and re-layouts: 5.97 us -> 4.86 us
  transfers between devices with their start and end apart: 5 -> 5, of which waited for: 2 -> 3; matrix products, arithmetic and copies ran while one was open for 9% -> 5% of each run, Pallas kernels for 0% -> 0%
where the time goes in v1:
time: 244 us; the launch traced here: 243 us
  waiting for transfers between devices  178 us (73%)
  other arithmetic  22 us (9%)
  between operations  14.4 us (6%)
  starting transfers between devices  10.1 us (4%)
  matrix products  10 us (4%)
  local copies, waits for them, and re-layouts  8.5 us (3%)
    all_gather x1, waiting for transfers between devices, body(): summed = jnp.sum(lax.all_gather(weight_part, 'tile'), axis=0)  175 us
    reduce_sum x1, other arithmetic, body(): summed = jnp.sum(lax.all_gather(weight_part, 'tile'), axis=0)  13.5 us
    ppermute x4, starting transfers between devices, from_behind(): lax.ppermute(value, axis, [(source, source + steps) for source in range(i...  10 us
  transfers between devices with their start and end apart: 5, of which 3 were waited for; matrix products, arithmetic and copies ran while one was open for 5% of the time, Pallas kernels for 0%

profile of v1, /device:TPU:0, one launch (start us, length us, event | category | flops | bytes accessed | tf_op | source)
XLA Modules:
  0.0 243.2 jit_solution(13276742248891391736)
XLA Ops:
  7.2 0.8 slice_bitcast_fusion.11
  8.1 2.4 collective-permute-start
  10.5 1.3 collective-permute-start.1
  11.8 1.3 fusion.14
  13.1 0.7 select_clamp_fusion
  13.9 0.7 broadcast_compare_fusion
  14.6 0.7 compare_convert_fusion
  15.7 0.6 gather_fusion
  16.9 1.2 pad_maximum_fusion
  19.3 0.5 fusion.9
  20.5 0.5 copy-done.1
  21.2 3.5 %fusion.6 = (bf16[6,16,16,256]{3,2,1,0:T(8,128)(2,1)S(1)}, bf16[6,16,16,256]{3,2,1,0:T(8,128)(2,1)}) fusion(bf16[6,16,16,256]{3,2,1,0:T(8,128)(2,1)S(1)} %copy-done.2, f32[6]{0:T(128)S(1)} %compare_convert_fusion, bf16[6,16,16,2304]{3,2,1,0:T(8,128)(2,1)S(1)} %slice_dynamic-update-slice_fusion.6, bf16[2304,256,1,1]{1,0,3,2:T(8,128)(2,1)S(1)} %bitcast.106), kind=kOutput, calls=%fused_computation.10 | convolution fusion | flops 1817837568 | bytes 10616856 | tf_op jit(solution)/shard_map/dot_general | solution.py:88
  24.8 3.5 %convolution_bitcast_fusion = f32[2304,256]{1,0:T(8,128)} fusion(bf16[6,16,16,2304]{3,2,1,0:T(8,128)(2,1)S(1)} %slice_dynamic-update-slice_fusion.6, bf16[6,16,16,256]{3,2,1,0:T(8,128)(2,1)S(1)} %get-tuple-element.4), kind=kOutput, calls=%fused_computation.2 | convolution fusion | flops 1811939328 | bytes 10223616 | tf_op jit(solution)/shard_map/dot_general | solution.py:99
  28.3 0.7 copy.89
  29.3 4.9 %collective-permute-start.2 = (bf16[6,16,256]{2,1,0:T(8,128)(2,1)S(1)}, bf16[6,16,256]{2,1,0:T(8,128)(2,1)S(1)}, u32[]{:S(2)}, u32[]{:S(2)}) collective-permute-start(bf16[6,16,256]{2,1,0:T(8,128)(2,1)S(1)} %get-tuple-element.12), channel_id=1, source_target_pairs={{0,1},{1,2},{2,3},{3,4},{4,5},{5,6},{6,7},{7,8},{8,9},{9,10},{10,1... | collective-permute-start | bytes 147464 | tf_op jit(solution)/shard_map/ppermute | solution.py:15
  34.2 1.5 collective-permute-start.3
  35.7 2.8 %collective-permute-done.3 = bf16[6,16,256]{2,1,0:T(8,128)(2,1)S(1)} collective-permute-done((bf16[6,16,256]{2,1,0:T(8,128)(2,1)S(1)}, bf16[6,16,256]{2,1,0:T(8,128)(2,1)S(1)}, u32[]{:S(2)}, u32[]{:S(2)}) %collective-permute-start.3) | collective-permute-done | bytes 49184 | tf_op jit(solution)/shard_map/ppermute | solution.py:15
  38.6 0.6 gather_fusion.1
  39.7 1.2 maximum_maximum_fusion.1
  41.6 0.5 fusion.8
  43.2 3.0 %multiply_convert_fusion = bf16[6,16,16,256]{3,2,1,0:T(8,128)(2,1)} fusion(bf16[6,16,16,2304]{3,2,1,0:T(8,128)(2,1)S(1)} %slice_dynamic-update-slice_fusion, bf16[2304,256,1,1]{1,0,3,2:T(8,128)(2,1)S(1)} %bitcast.107, f32[6]{0:T(128)S(1)} %compare_convert_fusion), kind=kOutput, calls=%fused_computation.11 | convolution fusion | flops 1812725760 | bytes 9043992 | tf_op jit(solution)/shard_map/dot_general | solution.py:111
  46.2 175.0 %all-gather.3.cloned.1.call-done = f32[36864,256]{1,0:T(8,128)} async-done(((f32[2304,256]{1,0:T(8,128)}), f32[36864,256]{1,0:T(8,128)}) %all-gather.3.cloned.1.call-update) | async-done | bytes 37748752 | tf_op jit(solution)/shard_map/all_gather | solution.py:143
  221.1 13.5 %reduce_sum.9 = f32[2304,256]{1,0:T(8,128)S(1)} reduce(f32[16,2304,256]{2,1,0:T(8,128)} %bitcast.102, f32[]{:T(128)} %constant.24.clone.1), dimensions={0}, to_apply=%region_0.2 | reduce | flops 8847360 | bytes 40108036 | tf_op jit(solution)/shard_map/reduce_sum | solution.py:143
  234.7 1.6 broadcast_multiply_fusion
  (57 shorter events, 5.8 us)
Async XLA Ops:
  7.2 214.0 %all-gather.3.cloned.1.call-start = ((), (), s32[]{:S(2)}) async-start(), calls=%async_computation | async-start | bytes 40108032 | tf_op jit(solution)/shard_map/all_gather | solution.py:143
  8.1 7.4 %collective-permute-start = (bf16[6,16,256]{2,1,0:T(8,128)(2,1)S(1)}, bf16[6,16,256]{2,1,0:T(8,128)(2,1)S(1)}, u32[]{:S(2)}, u32[]{:S(2)}) collective-permute-start(bf16[6,16,256]{2,1,0:T(8,128)(2,1)S(1)} %get-tuple-element.18), channel_id=1, source_target_pairs={{0,1},{1,2},{2,3},{3,4},{4,5},{5,6},{6,7},{7,8},{8,9},{9,10},{10,1... | collective-permute-start | bytes 147464 | tf_op jit(solution)/shard_map/ppermute | solution.py:15
  10.5 5.2 %collective-permute-start.1 = (bf16[6,16,256]{2,1,0:T(8,128)(2,1)S(1)}, bf16[6,16,256]{2,1,0:T(8,128)(2,1)S(1)}, u32[]{:S(2)}, u32[]{:S(2)}) collective-permute-start(bf16[6,16,256]{2,1,0:T(8,128)(2,1)S(1)} %get-tuple-element.17), channel_id=1, source_target_pairs={{1,0},{2,1},{3,2},{4,3},{5,4},{6,5},{7,6},{8,7},{9,8},{10,9},{11,1... | collective-permute-start | bytes 147464 | tf_op jit(solution)/shard_map/ppermute | solution.py:15
  15.2 1.7 copy-start
  19.8 1.3 copy-start.1
  19.8 1.5 copy-start.2
  29.3 6.4 %collective-permute-start.2 = (bf16[6,16,256]{2,1,0:T(8,128)(2,1)S(1)}, bf16[6,16,256]{2,1,0:T(8,128)(2,1)S(1)}, u32[]{:S(2)}, u32[]{:S(2)}) collective-permute-start(bf16[6,16,256]{2,1,0:T(8,128)(2,1)S(1)} %get-tuple-element.12), channel_id=1, source_target_pairs={{0,1},{1,2},{2,3},{3,4},{4,5},{5,6},{6,7},{7,8},{8,9},{9,10},{10,1... | collective-permute-start | bytes 147464 | tf_op jit(solution)/shard_map/ppermute | solution.py:15
  34.2 4.4 %collective-permute-start.3 = (bf16[6,16,256]{2,1,0:T(8,128)(2,1)S(1)}, bf16[6,16,256]{2,1,0:T(8,128)(2,1)S(1)}, u32[]{:S(2)}, u32[]{:S(2)}) collective-permute-start(bf16[6,16,256]{2,1,0:T(8,128)(2,1)S(1)} %get-tuple-element.11), channel_id=1, source_target_pairs={{1,0},{2,1},{3,2},{4,3},{5,4},{6,5},{7,6},{8,7},{9,8},{10,9},{11,1... | collective-permute-start | bytes 147464 | tf_op jit(solution)/shard_map/ppermute | solution.py:15
Sparse Core Ops, SparseCore 0:
  28.5 192.6 all-gather.2
